TPU v7x, 32 devices: a whole 2x2x4 slice. The times are simulated.
32 devices in a mesh: ctx: 4 (over z), rec: 8 (over y, x, core).
Axes of the slice: x: 2, y: 2, z: 4, core: 2. Of those that a mesh axis runs over, the one named last changes fastest.
Arguments:
- queries: bfloat16 [8, 1024, 1280], P('rec', 'ctx'), may hold values from -24 to 24
- video_keys: bfloat16 [8, 512, 1280], P('rec', 'ctx'), may hold values from -24 to 24
- video_values: bfloat16 [8, 512, 1280], P('rec', 'ctx'), may hold values from -6 to 6
- out_weight: bfloat16 [1280, 1280], replicated, may hold values from -0.15625 to 0.15625
- gate_logit: float32 [1], replicated, may hold values from 0.3 to 1.2
- row_grads: bfloat16 [16384, 1280], P(('ctx', 'rec')), may hold values from -6 to 6
- dest_device: int32 [16384], P(('ctx', 'rec')), may hold values from 0 to 31, as said below
- dest_row: int32 [16384], P(('ctx', 'rec')), may hold values from 0 to 255, as said below
- live_count: int32 [32], P(('ctx', 'rec')), may hold values from 0 to 512, as said below
Outputs:
- query_grads: bfloat16 [16384, 1280], P(('ctx', 'rec'))
- key_grads: bfloat16 [8, 512, 1280], P('rec', 'ctx')
- value_grads: bfloat16 [8, 512, 1280], P('rec', 'ctx')
- weight_grads: float32 [1280, 1280], P(('ctx', 'rec'))
- gate_grad: float32 [1], replicated
Inputs may be any that keep to these rules, and one draw needn't show every extreme that they name: `dest_device`: for the live slots of all devices together, each pair of owner device and audio row appears exactly once; the live slots of one device name one owner at most 16 times, and some device names each owner exactly 16 times. Slots that are not live hold 0. `dest_row`: slots that are not live hold 0. `live_count`: the live slots of a device are its first ones; the counts sum to 8192, and the largest is exactly 512.
All inputs are finite; a program needn't handle non-finite values.
Results may differ from a plain program's by a relative error of at most 0.012.
The roundings to bfloat16 on the way count: a program that leaves them out, or rounds other values in their place, can miss the bound.
Values may be sent and summed in bfloat16 or wider, within the bound.
No kernel may reach another device: no remote copies, remote signals or barrier semaphores. Data moves between devices by JAX's collectives and lax.ppermute only.
A program may use at most 192 MiB of HBM per device.

v0:
```python
import math
import jax
import jax.numpy as jnp
from jax import lax
from jax.sharding import PartitionSpec as P

HEADS = 20
HEAD_DIM = 64


def head_blocks(query_rows, keys_all, values_all, grad_attn):
    rows_q = query_rows.shape[0]
    rows_k = keys_all.shape[0]
    model_width = query_rows.shape[1]
    per_block = math.gcd(HEADS, 4)
    col_span = per_block * HEAD_DIM
    inv_root = HEAD_DIM ** (-0.5)
    attn_parts = []
    query_parts = []
    key_parts = []
    value_parts = []
    for block_idx in range(model_width // col_span):
        first_col = block_idx * col_span
        query_heads = query_rows[:, first_col : first_col + col_span].reshape(
            rows_q, per_block, HEAD_DIM
        )
        key_heads = keys_all[:, first_col : first_col + col_span].reshape(
            rows_k, per_block, HEAD_DIM
        )
        value_heads = values_all[:, first_col : first_col + col_span].reshape(
            rows_k, per_block, HEAD_DIM
        )
        grad_heads = grad_attn[:, first_col : first_col + col_span].reshape(
            rows_q, per_block, HEAD_DIM
        )
        scores = (
            jnp.einsum("ahd,vhd->hav", query_heads, key_heads, preferred_element_type=jnp.float32)
            * inv_root
        )
        row_peak = jnp.max(scores, axis=-1, keepdims=True)
        shifted = jnp.exp(scores - row_peak)
        softmax_w = shifted / jnp.sum(shifted, axis=-1, keepdims=True)
        probs_low = softmax_w.astype(jnp.bfloat16)
        attn_low = jnp.einsum(
            "hav,vhd->ahd", probs_low, value_heads, preferred_element_type=jnp.float32
        ).astype(jnp.bfloat16)
        row_delta = jnp.einsum(
            "ahd,ahd->ha", grad_heads, attn_low, preferred_element_type=jnp.float32
        )
        dprob = jnp.einsum(
            "ahd,vhd->hav", grad_heads, value_heads, preferred_element_type=jnp.float32
        )
        dscore = (softmax_w * (dprob - row_delta[:, :, None])).astype(jnp.bfloat16)
        query_part = (
            jnp.einsum("hav,vhd->ahd", dscore, key_heads, preferred_element_type=jnp.float32)
            * inv_root
        )
        key_part = (
            jnp.einsum("hav,ahd->vhd", dscore, query_heads, preferred_element_type=jnp.float32)
            * inv_root
        )
        value_part = jnp.einsum(
            "hav,ahd->vhd", probs_low, grad_heads, preferred_element_type=jnp.float32
        )
        attn_parts.append(attn_low.reshape(rows_q, col_span))
        query_parts.append(query_part.reshape(rows_q, col_span))
        key_parts.append(key_part.reshape(rows_k, col_span).astype(jnp.bfloat16))
        value_parts.append(value_part.reshape(rows_k, col_span).astype(jnp.bfloat16))
    return (
        jnp.concatenate(attn_parts, axis=1),
        jnp.concatenate(query_parts, axis=1),
        jnp.concatenate(key_parts, axis=1),
        jnp.concatenate(value_parts, axis=1),
    )


def local(
    queries,
    video_keys,
    video_values,
    out_weight,
    gate_logit,
    row_grads,
    dest_device,
    dest_row,
    live_count,
):
    ctx_count = lax.axis_size("ctx")
    rec_count = lax.axis_size("rec")
    all_count = ctx_count * rec_count
    slot_count = row_grads.shape[0]
    pair_cap = slot_count // all_count
    audio_rows = queries.shape[1]
    model_width = out_weight.shape[0]
    slot_ids = jnp.arange(slot_count, dtype=jnp.int32)
    is_live = slot_ids < live_count[0]
    owner_ids = jnp.arange(all_count, dtype=jnp.int32)
    owner_hot = jnp.logical_and(
        dest_device[:, None] == owner_ids[None, :], is_live[:, None]
    ).astype(jnp.bfloat16)
    earlier = (slot_ids[None, :] < slot_ids[:, None]).astype(jnp.bfloat16)
    before = jnp.dot(earlier, owner_hot, preferred_element_type=jnp.float32)
    bucket_rank = jnp.sum(before * owner_hot.astype(jnp.float32), axis=1).astype(jnp.int32)
    slot_target = jnp.where(is_live, dest_device * pair_cap + bucket_rank, slot_count)
    send_grads = (
        jnp.zeros((slot_count, model_width), jnp.bfloat16)
        .at[slot_target]
        .set(row_grads, mode="drop")
    )
    send_index = (
        jnp.full((slot_count,), audio_rows, jnp.int32).at[slot_target].set(dest_row, mode="drop")
    )
    recv_grads, recv_index = (
        lax.all_to_all(
            send_grads.reshape(all_count, pair_cap, model_width),
            ("ctx", "rec"),
            split_axis=0,
            concat_axis=0,
            tiled=True,
        ),
        lax.all_to_all(
            send_index.reshape(all_count, pair_cap),
            ("ctx", "rec"),
            split_axis=0,
            concat_axis=0,
            tiled=True,
        ),
    )
    recv_grads = recv_grads.reshape(slot_count, model_width)
    recv_index = recv_index.reshape(slot_count)
    grad_rows = (
        jnp.zeros((audio_rows + 1, model_width), jnp.bfloat16)
        .at[recv_index]
        .set(recv_grads)[:audio_rows]
    )
    keys_all, values_all = (
        lax.all_gather(video_keys, "ctx", axis=1, tiled=True),
        lax.all_gather(video_values, "ctx", axis=1, tiled=True),
    )
    gate_value = jnp.tanh(gate_logit[0])
    upstream = lax.dot_general(
        grad_rows, out_weight, (((1,), (1,)), ((), ())), preferred_element_type=jnp.float32
    )
    grad_attn = (gate_value * upstream).astype(jnp.bfloat16)
    attn_low, query_grad, key_term, value_term = head_blocks(
        queries[0], keys_all[0], values_all[0], grad_attn
    )
    key_sum, value_sum = (
        lax.psum_scatter(key_term[None], "ctx", scatter_dimension=1, tiled=True).astype(
            jnp.float32
        ),
        lax.psum_scatter(value_term[None], "ctx", scatter_dimension=1, tiled=True).astype(
            jnp.float32
        ),
    )
    weight_grad = lax.psum_scatter(
        gate_value
        * lax.dot_general(
            grad_rows, attn_low, (((0,), (0,)), ((), ())), preferred_element_type=jnp.float32
        ),
        ("ctx", "rec"),
        scatter_dimension=0,
        tiled=True,
    )
    shrink = 1.0 - gate_value * gate_value
    gate_total = lax.psum(jnp.sum(upstream * attn_low.astype(jnp.float32)), ("ctx", "rec"))
    gate_grad = shrink * gate_total
    padded_grad = jnp.concatenate(
        [query_grad.astype(jnp.bfloat16), jnp.zeros((1, model_width), jnp.bfloat16)], axis=0
    )
    back_rows = padded_grad[recv_index]
    returned = lax.all_to_all(
        back_rows.reshape(all_count, pair_cap, model_width),
        ("ctx", "rec"),
        split_axis=0,
        concat_axis=0,
        tiled=True,
    )
    returned = returned.reshape(slot_count, model_width)
    picked = returned[jnp.minimum(slot_target, slot_count - 1)]
    query_grads = jnp.where(is_live[:, None], picked, jnp.zeros((), jnp.bfloat16))
    return (
        query_grads,
        key_sum.astype(jnp.bfloat16),
        value_sum.astype(jnp.bfloat16),
        weight_grad,
        gate_grad.reshape(1),
    )


def solution(mesh):
    in_specs = (
        P("rec", "ctx", None),
        P("rec", "ctx", None),
        P("rec", "ctx", None),
        P(),
        P(),
        P(("ctx", "rec"), None),
        P(("ctx", "rec")),
        P(("ctx", "rec")),
        P(("ctx", "rec")),
    )
    out_specs = (
        P(("ctx", "rec"), None),
        P("rec", "ctx", None),
        P("rec", "ctx", None),
        P(("ctx", "rec"), None),
        P(),
    )
    return jax.shard_map(local, mesh=mesh, in_specs=in_specs, out_specs=out_specs, check_vma=False)
```

profile of v0, /device:TPU:0, one launch (start us, length us, event | category | flops | bytes accessed | tf_op | source)
XLA Modules:
  0.0 445.9 jit_solution(16039810445099604421)
XLA Ops:
  11.6 2.6 scatter_custom_fusion
  14.9 7.3 %all-to-all-start = ((s32[32,1,16]{2,1,0:T(1,128)}), s32[32,1,16]{2,1,0:T(1,128)S(1)}, u32[]{:S(2)}, u32[]{:S(2)}) async-start(s32[32,1,16]{2,1,0:T(1,128)} %bitcast.16), calls=%async_computation | async-start | bytes 32768 | tf_op jit(solution)/shard_map/all_to_all | solution.py:121
  31.3 4.7 %scatter_custom_fusion.1 = bf16[512,1280]{1,0:T(8,128)(2,1)} fusion(s32[512]{0:T(512)} %copy-done.28, bf16[512,1280]{1,0:T(8,128)(2,1)} %param.14, bf16[]{:T(256)} %constant.14.clone.1), kind=kCustom, calls=%fused_computation.82 | custom fusion | bytes 1311232 | tf_op jit(solution)/shard_map/scatter | solution.py:108
  36.0 5.9 %all-to-all-start.1 = ((bf16[32,16,1280]{2,1,0:T(8,128)(2,1)}), bf16[32,16,1280]{2,1,0:T(8,128)(2,1)}, u32[]{:S(2)}, u32[]{:S(2)}) async-start(bf16[32,16,1280]{2,1,0:T(8,128)(2,1)} %bitcast.197), calls=%async_computation.1 | async-start | bytes 2621440 | tf_op jit(solution)/shard_map/all_to_all | solution.py:114
  49.5 45.7 %all-gather.5.cloned.1.call-done = bf16[1,512,1280]{2,1,0:T(8,128)(2,1)} async-done(((bf16[1,128,1280]{2,1,0:T(8,128)(2,1)}), bf16[1,512,1280]{2,1,0:T(8,128)(2,1)}) %all-gather.5.cloned.1.call-update) | async-done | bytes 1310736 | tf_op jit(solution)/shard_map/all_gather | solution.py:138
  95.2 2.4 fusion.66
  112.8 3.2 fusion.69
  120.0 3.1 fusion.70
  127.2 3.2 fusion.71
  135.9 3.8 fusion.72
  145.3 3.8 fusion.73
  162.7 4.3 scatter_custom_fusion.2
  167.0 3.0 multiply_reduce_fusion.5
  250.3 5.1 %convolution_multiply_fusion = f32[1280,1280]{1,0:T(8,128)} fusion(bf16[256,1280]{1,0:T(8,128)(2,1)} %constant_dynamic-update-slice_fusion.15, f32[]{:T(128)} %bitcast.15, bf16[257,1280]{1,0:T(8,128)(2,1)} %scatter_custom_fusion.2), kind=kOutput, calls=%fused_computation.10 | convolution fusion | flops 840499200 | bytes 7864832 | tf_op jit(solution)/shard_map/dot_general | solution.py:158
  256.3 2.3 fusion.19
  260.3 2.5 fusion.18
  264.5 2.4 fusion.17
  268.5 2.4 fusion.16
  280.5 5.1 %gather_fusion = bf16[512,1280]{1,0:T(8,128)(2,1)} fusion(bf16[257,1280]{1,0:T(8,128)(2,1)} %concatenate.17, s32[1024]{0:T(1024)S(1)} %pad_clamp_fusion.1), kind=kCustom, calls=%fused_computation | custom fusion | bytes 2623488 | tf_op jit(solution)/shard_map/gather | solution.py:171
  285.6 3.8 all-to-all-start.2
  289.5 59.1 %psum.7 = f32[]{:T(128)} all-reduce(f32[]{:T(128)} %get-tuple-element.5), channel_id=1, replica_groups=mesh['ctx'=4,'rec'=8] {'ctx','rec'}, use_global_device_ids=true, to_apply=%region_18.19 | all-reduce | flops 1 | bytes 8 | tf_op jit(solution)/shard_map/psum | solution.py:166
  349.2 5.4 %gather_fusion.1 = bf16[512,1280]{1,0:T(8,128)(2,1)} fusion(bf16[512,1280]{1,0:T(8,128)(2,1)} %bitcast.70, s32[1024]{0:T(1024)S(1)} %pad_clamp_fusion), kind=kCustom, calls=%fused_computation.1 | custom fusion | bytes 2623488 | tf_op jit(solution)/shard_map/gather | solution.py:180
  354.7 2.5 broadcast_select_fusion
  357.2 81.1 %reduce-scatter.8.cloned.1.call-done = f32[40,1280]{1,0:T(8,128)} async-done(((f32[1280,1280]{1,0:T(8,128)}), f32[40,1280]{1,0:T(8,128)}) %reduce-scatter.8.cloned.1.call-update) | async-done | bytes 204816 | tf_op jit(solution)/shard_map/reduce_scatter | solution.py:156
  (183 shorter events, 164.1 us)
Async XLA Ops:
  7.2 159.8 %copy-start = (bf16[1280,1280]{1,0:T(8,128)(2,1)S(1)}, bf16[1280,1280]{1,0:T(8,128)(2,1)}, u32[]{:S(2)}) copy-start(bf16[1280,1280]{1,0:T(8,128)(2,1)} %param.12) | copy-start | bytes 9830404
  7.2 38.3 %all-gather.3.cloned.1.call-start = ((), (), s32[]{:S(2)}) async-start(), calls=%async_computation.6 | async-start | bytes 1638400 | tf_op jit(solution)/shard_map/all_gather | solution.py:137
  7.9 87.3 %all-gather.5.cloned.1.call-start = ((), (), s32[]{:S(2)}) async-start(), calls=%async_computation.7 | async-start | bytes 1638400 | tf_op jit(solution)/shard_map/all_gather | solution.py:138
  11.6 10.6 %copy-start.28 = (s32[512]{0:T(512)}, s32[512]{0:T(512)S(1)}, u32[]{:S(2)}) copy-start(s32[512]{0:T(512)S(1)} %get-tuple-element.28) | copy-start | bytes 6148
  14.9 21.1 %all-to-all-start = ((s32[32,1,16]{2,1,0:T(1,128)}), s32[32,1,16]{2,1,0:T(1,128)S(1)}, u32[]{:S(2)}, u32[]{:S(2)}) async-start(s32[32,1,16]{2,1,0:T(1,128)} %bitcast.16), calls=%async_computation | async-start | bytes 32768 | tf_op jit(solution)/shard_map/all_to_all | solution.py:121
  36.0 126.7 %all-to-all-start.1 = ((bf16[32,16,1280]{2,1,0:T(8,128)(2,1)}), bf16[32,16,1280]{2,1,0:T(8,128)(2,1)}, u32[]{:S(2)}, u32[]{:S(2)}) async-start(bf16[32,16,1280]{2,1,0:T(8,128)(2,1)} %bitcast.197), calls=%async_computation.1 | async-start | bytes 2621440 | tf_op jit(solution)/shard_map/all_to_all | solution.py:114
  41.9 315.2 %reduce-scatter.6.cloned.1.call-start = ((), (), s32[]{:S(2)}) async-start(), calls=%async_computation.9 | async-start | bytes 1638400 | tf_op jit(solution)/shard_map/reduce_scatter | solution.py:152
  116.0 2.9 copy-start.16
  116.0 4.1 copy-start.22
  123.1 2.9 copy-start.17
  175.8 3.3 copy-start.26
  188.6 3.4 copy-start.25
  215.5 7.0 %copy-start.13 = (bf16[512,256]{1,0:T(8,128)(2,1)S(1)}, bf16[512,256]{1,0:T(8,128)(2,1)}, u32[]{:S(2)}) copy-start(bf16[512,256]{1,0:T(8,128)(2,1)} %copy.134) | copy-start | bytes 786436
  223.2 134.0 %reduce-scatter.4.cloned.1.call-start = ((), (), s32[]{:S(2)}) async-start(), calls=%async_computation.8 | async-start | bytes 1638400 | tf_op jit(solution)/shard_map/reduce_scatter | solution.py:149
  223.3 3.3 copy-start.24
  230.3 3.4 copy-start.23
  230.3 6.2 %copy-start.11 = (bf16[256,256]{0,1:T(8,128)(2,1)S(1)}, bf16[256,256]{0,1:T(8,128)(2,1)}, u32[]{:S(2)}) copy-start(bf16[256,256]{0,1:T(8,128)(2,1)} %copy.102) | copy-start | bytes 393220
  236.5 3.2 copy-start.21
  239.7 9.7 %copy-start.12 = (bf16[512,256]{1,0:T(8,128)(2,1)S(1)}, bf16[512,256]{1,0:T(8,128)(2,1)}, u32[]{:S(2)}) copy-start(bf16[512,256]{1,0:T(8,128)(2,1)} %copy.129) | copy-start | bytes 786436
  250.2 188.1 %reduce-scatter.8.cloned.1.call-start = ((), (), s32[]{:S(2)}) async-start(), calls=%async_computation.10 | async-start | bytes 6758400 | tf_op jit(solution)/shard_map/reduce_scatter | solution.py:156
  262.8 9.7 %copy-start.15 = (bf16[512,256]{0,1:T(8,128)(2,1)S(1)}, bf16[512,256]{0,1:T(8,128)(2,1)}, u32[]{:S(2)}) copy-start(bf16[512,256]{0,1:T(8,128)(2,1)} %copy.100) | copy-start | bytes 786436
  285.6 3.9 copy-start.27
  285.6 63.6 %all-to-all-start.2 = ((bf16[32,16,1280]{2,1,0:T(8,128)(2,1)}), bf16[32,16,1280]{2,1,0:T(8,128)(2,1)}, u32[]{:S(2)}, u32[]{:S(2)}) async-start(bf16[32,16,1280]{2,1,0:T(8,128)(2,1)} %bitcast.196), calls=%async_computation.2 | async-start | bytes 2621440 | tf_op jit(solution)/shard_map/all_to_all | solution.py:172
  349.2 5.4 %copy-start.30 = (pred[512]{0:T(512)(128)(4,1)S(1)}, pred[512]{0:T(512)(128)(4,1)}, u32[]{:S(2)}) copy-start(pred[512]{0:T(512)(128)(4,1)} %copy-done.29) | copy-start | bytes 1540
  (15 other events, 21.8 us)
Sparse Core Ops, SparseCore 0:
  9.6 35.8 all-gather.2
  47.0 48.1 all-gather.4
  223.3 30.4 reduce-scatter.5
  256.5 29.9 reduce-scatter.3
  289.3 148.9 reduce-scatter.7
where the time goes:
time: 449 us; the launch traced here: 446 us
  local copies, waits for them, and re-layouts  134 us (30%)
  waiting for transfers between devices  130 us (29%)
  matrix products  70 us (16%)
  blocking collectives  59.1 us (13%)
  other arithmetic  18.4 us (4%)
  starting transfers between devices  17.5 us (4%)
  between operations  17.3 us (4%)
    reduce_scatter x1, waiting for transfers between devices, local(): lax.psum_scatter(gate_value * lax.dot_general(grad_rows, attn_low, (((0,)...  81.1 us
    psum x1, blocking collectives, local(): lax.psum(jnp.sum(upstream * attn_low.astype(jnp.float32)), ('ctx', 'rec'))  59.1 us
    all_gather x1, waiting for transfers between devices, local(): lax.all_gather(video_values, 'ctx', axis=1, tiled=True)  45.7 us
    unnamed x78, local copies, waits for them, and re-layouts  33.9 us
    sub x5, matrix products, head_blocks(): shifted = jnp.exp(scores - row_peak)  17 us
    dot_general x5, matrix products, head_blocks(): jnp.einsum('hav,vhd->ahd', dscore, key_heads, preferred_element_type=jnp....  11.9 us
    dot_general x5, matrix products, head_blocks(): jnp.einsum('hav,ahd->vhd', probs_low, grad_heads, preferred_element_type=...  11.5 us
    dot_general x5, matrix products, head_blocks(): jnp.einsum('ahd,vhd->hav', grad_heads, value_heads, preferred_element_typ...  11.4 us
  transfers between devices with their start and end apart: 8, of which 3 were waited for; matrix products, arithmetic and copies ran while one was open for 34% of the time, Pallas kernels for 0%

commit v1 on v0

--- a/solution.py
+++ b/solution.py
@@ -133,9 +133,29 @@
         .at[recv_index]
         .set(recv_grads)[:audio_rows]
     )
+
+    def hold_ladders(block_here, a_name):
+        workers = lax.axis_size(a_name)
+        rack = []
+        for pp in tuple(range(workers)):
+            rack.append((pp, (pp + 1) % workers))
+        rows = []
+        for pp in tuple(range(workers)):
+            rows.append((pp, (pp - 1) % workers))
+        val, met_up = ([block_here], [block_here])
+        for _ in range(workers // 2):
+            base_arr = lax.ppermute(val[-1], a_name, rack)
+            val.append(base_arr)
+        for _ in tuple(range((workers - 1) // 2)):
+            block_now = lax.ppermute(met_up[-1], a_name, rows)
+            met_up.append(block_now)
+        y2 = jnp.concatenate([*val[::-1], *met_up[1:]], axis=1)
+        t1 = lax.axis_index(a_name)
+        return jnp.roll(y2, shift=(t1 - workers // 2) * block_here.shape[1], axis=1)
+
     keys_all, values_all = (
         lax.all_gather(video_keys, "ctx", axis=1, tiled=True),
-        lax.all_gather(video_values, "ctx", axis=1, tiled=True),
+        hold_ladders(video_values, "ctx"),
     )
     gate_value = jnp.tanh(gate_logit[0])
     upstream = lax.dot_general(

time: 449 us -> 376 us (0.84)
  waiting for transfers between devices: 130 us -> 96.1 us
  local copies, waits for them, and re-layouts: 134 us -> 106 us
  matrix products: 70 us -> 54.3 us
  starting transfers between devices: 17.5 us -> 22.8 us
    all_gather x1 -> x0, waiting for transfers between devices: 45.7 us -> none  [local(): lax.all_gather(video_values, 'ctx', axis=1, tiled=True)]
    reduce_scatter x1, waiting for transfers between devices: 81.1 us -> 91.2 us  [local(): lax.psum_scatter(gate_value * lax.dot_general(grad_rows, attn_low, (((0,)...]
    ppermute x0 -> x3, starting transfers between devices: none -> 6.99 us  [the longest x2 4.9 us: hold_ladders(): base_arr = lax.ppermute(val[-1], a_name, rack)]
    dot_general x5, matrix products: 11.5 us -> 4.58 us  [head_blocks(): jnp.einsum('hav,ahd->vhd', probs_low, grad_heads, preferred_element_type=...]
    slice x6, local copies, waits for them, and re-layouts: 9.11 us -> 3.95 us  [head_blocks(): grad_attn[:, first_col:first_col + col_span]]
    convert_element_type x5, local copies, waits for them, and re-layouts: 8.96 us -> 4.36 us  [head_blocks(): value_part.reshape(rows_k, col_span).astype(jnp.bfloat16)]
    unnamed x78 -> x121, local copies, waits for them, and re-layouts: 33.9 us -> 29.5 us
  transfers between devices with their start and end apart: 8 -> 10, of which waited for: 3 -> 3; matrix products, arithmetic and copies ran while one was open for 34% -> 38% of each run, Pallas kernels for 0% -> 0%
where the time goes in v1:
time: 376 us; the launch traced here: 374 us
  local copies, waits for them, and re-layouts  106 us (28%)
  waiting for transfers between devices  96.1 us (26%)
  blocking collectives  58.4 us (16%)
  matrix products  54.3 us (14%)
  starting transfers between devices  22.8 us (6%)
  other arithmetic  18.7 us (5%)
  between operations  17.7 us (5%)
    reduce_scatter x1, waiting for transfers between devices, local(): lax.psum_scatter(gate_value * lax.dot_general(grad_rows, attn_low, (((0,)...  91.2 us
    psum x1, blocking collectives, local(): lax.psum(jnp.sum(upstream * attn_low.astype(jnp.float32)), ('ctx', 'rec'))  58.4 us
    unnamed x121, local copies, waits for them, and re-layouts  29.5 us
    sub x5, matrix products, head_blocks(): shifted = jnp.exp(scores - row_peak)  15.6 us
    dot_general x5, matrix products, head_blocks(): jnp.einsum('ahd,vhd->hav', grad_heads, value_heads, preferred_element_typ...  10.5 us
    slice x6, local copies, waits for them, and re-layouts, head_blocks(): keys_all[:, first_col:first_col + col_span]  10.3 us
    convert_element_type x5, other arithmetic, head_blocks(): probs_low = softmax_w.astype(jnp.bfloat16)  9.24 us
    slice x6, local copies, waits for them, and re-layouts, head_blocks(): values_all[:, first_col:first_col + col_span]  9.01 us
  transfers between devices with their start and end apart: 10, of which 3 were waited for; matrix products, arithmetic and copies ran while one was open for 38% of the time, Pallas kernels for 0%

profile of v1, /device:TPU:0, one launch (start us, length us, event | category | flops | bytes accessed | tf_op | source)
XLA Modules:
  0.0 373.9 jit_solution(13959999925589503330)
XLA Ops:
  7.2 3.1 collective-permute-start
  15.4 2.6 scatter_custom_fusion
  18.7 4.2 %all-to-all-start = ((s32[32,1,16]{2,1,0:T(1,128)}), s32[32,1,16]{2,1,0:T(1,128)S(1)}, u32[]{:S(2)}, u32[]{:S(2)}) async-start(s32[32,1,16]{2,1,0:T(1,128)} %bitcast.16), calls=%async_computation | async-start | bytes 32768 | tf_op jit(solution)/shard_map/all_to_all | solution.py:121
  33.8 4.7 %scatter_custom_fusion.1 = bf16[512,1280]{1,0:T(8,128)(2,1)} fusion(s32[512]{0:T(512)} %copy-done.46, bf16[512,1280]{1,0:T(8,128)(2,1)} %param.14, bf16[]{:T(256)} %constant.19.clone.1), kind=kCustom, calls=%fused_computation.83 | custom fusion | bytes 1311232 | tf_op jit(solution)/shard_map/scatter | solution.py:108
  38.5 4.2 %all-to-all-done = s32[32,1,16]{2,1,0:T(1,128)S(1)} async-done(((s32[32,1,16]{2,1,0:T(1,128)}), s32[32,1,16]{2,1,0:T(1,128)S(1)}, u32[]{:S(2)}, u32[]{:S(2)}) %all-to-all-start) | async-done | bytes 2080 | tf_op jit(solution)/shard_map/all_to_all | solution.py:121
  42.7 3.4 all-to-all-start.1
  67.7 3.2 fusion.70
  76.8 3.1 fusion.69
  85.7 3.1 fusion.71
  94.8 3.1 fusion.72
  103.7 3.2 fusion.73
  118.9 4.3 %scatter_custom_fusion.2 = bf16[257,1280]{1,0:T(8,128)(2,1)} fusion(s32[512]{0:T(512)S(1)} %bitcast.263, bf16[512,1280]{1,0:T(8,128)(2,1)} %bitcast.19, bf16[]{:T(256)} %constant.19.clone.1), kind=kCustom, calls=%fused_computation.88 | custom fusion | bytes 658432 | tf_op jit(solution)/shard_map/scatter | solution.py:134
  123.2 3.1 multiply_reduce_fusion.5
  153.4 2.3 multiply_convert_fusion.2
  159.5 2.3 multiply_convert_fusion.1
  178.4 5.1 %convolution_multiply_fusion = f32[1280,1280]{1,0:T(8,128)} fusion(bf16[256,1280]{1,0:T(8,128)(2,1)} %constant_dynamic-update-slice_fusion.23, f32[]{:T(128)} %bitcast.15, bf16[257,1280]{1,0:T(8,128)(2,1)} %scatter_custom_fusion.2), kind=kOutput, calls=%fused_computation.10 | convolution fusion | flops 840499200 | bytes 7864832 | tf_op jit(solution)/shard_map/dot_general | solution.py:178
  184.4 2.3 fusion.19
  187.8 2.4 fusion.18
  197.1 2.9 gather_fusion
  199.9 7.8 %all-to-all-start.2 = ((bf16[32,16,1280]{2,1,0:T(8,128)(2,1)}), bf16[32,16,1280]{2,1,0:T(8,128)(2,1)}, u32[]{:S(2)}, u32[]{:S(2)}) async-start(bf16[32,16,1280]{2,1,0:T(8,128)(2,1)} %bitcast.69), calls=%async_computation.2 | async-start | bytes 2621440 | tf_op jit(solution)/shard_map/all_to_all | solution.py:192
  207.8 58.4 %psum.7 = f32[]{:T(128)} all-reduce(f32[]{:T(128)} %get-tuple-element.5), channel_id=1, replica_groups=mesh['ctx'=4,'rec'=8] {'ctx','rec'}, use_global_device_ids=true, to_apply=%region_18.19 | all-reduce | flops 1 | bytes 8 | tf_op jit(solution)/shard_map/psum | solution.py:186
  266.9 5.5 %gather_fusion.1 = bf16[512,1280]{1,0:T(8,128)(2,1)} fusion(bf16[512,1280]{1,0:T(8,128)(2,1)} %bitcast.70, s32[1024]{0:T(1024)S(1)} %pad_clamp_fusion), kind=kCustom, calls=%fused_computation.1 | custom fusion | bytes 2623488 | tf_op jit(solution)/shard_map/gather | solution.py:200
  272.5 2.5 broadcast_select_fusion
  275.0 91.2 %reduce-scatter.8.cloned.1.call-done = f32[40,1280]{1,0:T(8,128)} async-done(((f32[1280,1280]{1,0:T(8,128)}), f32[40,1280]{1,0:T(8,128)}) %reduce-scatter.8.cloned.1.call-update) | async-done | bytes 204816 | tf_op jit(solution)/shard_map/reduce_scatter | solution.py:176
  (231 shorter events, 128.3 us)
Async XLA Ops:
  7.2 116.0 %copy-start = (bf16[1280,1280]{1,0:T(8,128)(2,1)S(1)}, bf16[1280,1280]{1,0:T(8,128)(2,1)}, u32[]{:S(2)}) copy-start(bf16[1280,1280]{1,0:T(8,128)(2,1)} %param.12) | copy-start | bytes 9830404
  7.2 57.4 %all-gather.2.cloned.1.call-start = ((), (), s32[]{:S(2)}) async-start(), calls=%async_computation.6 | async-start | bytes 1638400 | tf_op jit(solution)/shard_map/all_gather | solution.py:157
  7.2 15.7 %collective-permute-start = (bf16[1,128,1280]{2,1,0:T(8,128)(2,1)}, bf16[1,128,1280]{2,1,0:T(8,128)(2,1)}, u32[]{:S(2)}, u32[]{:S(2)}) collective-permute-start(bf16[1,128,1280]{2,1,0:T(8,128)(2,1)} %param.11), channel_id=1, source_target_pairs={{0,8},{8,16},{16,24},{24,0},{1,9},{9,17},{17,25},{25,1},{2,10},{10... | collective-permute-start | bytes 983048 | tf_op jit(solution)/shard_map/ppermute | solution.py:147
  10.3 40.4 %collective-permute-start.2 = (bf16[1,128,1280]{2,1,0:T(8,128)(2,1)}, bf16[1,128,1280]{2,1,0:T(8,128)(2,1)}, u32[]{:S(2)}, u32[]{:S(2)}) collective-permute-start(bf16[1,128,1280]{2,1,0:T(8,128)(2,1)} %param.11), channel_id=1, source_target_pairs={{0,24},{8,0},{16,8},{24,16},{1,25},{9,1},{17,9},{25,17},{2,26},{10... | collective-permute-start | bytes 983048 | tf_op jit(solution)/shard_map/ppermute | solution.py:150
  15.4 9.3 %copy-start.46 = (s32[512]{0:T(512)}, s32[512]{0:T(512)S(1)}, u32[]{:S(2)}) copy-start(s32[512]{0:T(512)S(1)} %get-tuple-element.28) | copy-start | bytes 6148
  18.7 24.0 %all-to-all-start = ((s32[32,1,16]{2,1,0:T(1,128)}), s32[32,1,16]{2,1,0:T(1,128)S(1)}, u32[]{:S(2)}, u32[]{:S(2)}) async-start(s32[32,1,16]{2,1,0:T(1,128)} %bitcast.16), calls=%async_computation | async-start | bytes 32768 | tf_op jit(solution)/shard_map/all_to_all | solution.py:121
  22.9 24.7 %collective-permute-start.1 = (bf16[1,128,1280]{2,1,0:T(8,128)(2,1)}, bf16[1,128,1280]{2,1,0:T(8,128)(2,1)}, u32[]{:S(2)}, u32[]{:S(2)}) collective-permute-start(bf16[1,128,1280]{2,1,0:T(8,128)(2,1)} %collective-permute-done), channel_id=1, source_target_pairs={{0,8},{8,16},{16,24},{24,0},{1,9},{9,17},{17,25},{25,1},{2,10},{10... | collective-permute-start | bytes 983048 | tf_op jit(solution)/shard_map/ppermute | solution.py:147
  42.7 76.2 %all-to-all-start.1 = ((bf16[32,16,1280]{2,1,0:T(8,128)(2,1)}), bf16[32,16,1280]{2,1,0:T(8,128)(2,1)}, u32[]{:S(2)}, u32[]{:S(2)}) async-start(bf16[32,16,1280]{2,1,0:T(8,128)(2,1)} %bitcast.199), calls=%async_computation.1 | async-start | bytes 2621440 | tf_op jit(solution)/shard_map/all_to_all | solution.py:114
  46.1 229.0 %reduce-scatter.6.cloned.1.call-start = ((), (), s32[]{:S(2)}) async-start(), calls=%async_computation.8 | async-start | bytes 1638400 | tf_op jit(solution)/shard_map/reduce_scatter | solution.py:172
  47.6 6.1 %copy-start.15 = (bf16[1,128,1280]{2,1,0:T(8,128)(2,1)S(1)}, bf16[1,128,1280]{2,1,0:T(8,128)(2,1)}, u32[]{:S(2)}) copy-start(bf16[1,128,1280]{2,1,0:T(8,128)(2,1)} %param.11) | copy-start | bytes 983044
  74.2 7.5 %copy-start.16 = (bf16[4,64,256]{2,1,0:T(8,128)(2,1)}, bf16[4,64,256]{2,1,0:T(8,128)(2,1)S(1)}, u32[]{:S(2)}) copy-start(bf16[4,64,256]{2,1,0:T(8,128)(2,1)S(1)} %convolution_convert_fusion.8) | copy-start | bytes 393220
  79.8 5.9 %copy-start.38 = (bf16[256,256]{0,1:T(8,128)(2,1)S(1)}, bf16[256,256]{0,1:T(8,128)(2,1)}, u32[]{:S(2)}) copy-start(bf16[256,256]{0,1:T(8,128)(2,1)} %copy.103) | copy-start | bytes 393220
  83.2 7.5 %copy-start.22 = (bf16[4,64,256]{2,1,0:T(8,128)(2,1)}, bf16[4,64,256]{2,1,0:T(8,128)(2,1)S(1)}, u32[]{:S(2)}) copy-start(bf16[4,64,256]{2,1,0:T(8,128)(2,1)S(1)} %convolution_convert_fusion.9) | copy-start | bytes 393220
  88.9 5.9 %copy-start.36 = (bf16[256,256]{0,1:T(8,128)(2,1)S(1)}, bf16[256,256]{0,1:T(8,128)(2,1)}, u32[]{:S(2)}) copy-start(bf16[256,256]{0,1:T(8,128)(2,1)} %copy.107) | copy-start | bytes 393220
  92.2 7.5 %copy-start.19 = (bf16[4,64,256]{2,1,0:T(8,128)(2,1)}, bf16[4,64,256]{2,1,0:T(8,128)(2,1)S(1)}, u32[]{:S(2)}) copy-start(bf16[4,64,256]{2,1,0:T(8,128)(2,1)S(1)} %convolution_convert_fusion.7) | copy-start | bytes 393220
  129.1 8.1 %copy-start.5 = (bf16[4,256,512]{2,1,0:T(8,128)(2,1)S(1)}, bf16[4,256,512]{2,1,0:T(8,128)(2,1)}, u32[]{:S(2)}) copy-start(bf16[4,256,512]{2,1,0:T(8,128)(2,1)} %copy-done.4) | copy-start | bytes 3145732
  130.8 9.5 %copy-start.7 = (bf16[4,256,512]{2,1,0:T(8,128)(2,1)S(1)}, bf16[4,256,512]{2,1,0:T(8,128)(2,1)}, u32[]{:S(2)}) copy-start(bf16[4,256,512]{2,1,0:T(8,128)(2,1)} %copy-done.6) | copy-start | bytes 3145732
  147.3 127.7 %reduce-scatter.4.cloned.1.call-start = ((), (), s32[]{:S(2)}) async-start(), calls=%async_computation.7 | async-start | bytes 1638400 | tf_op jit(solution)/shard_map/reduce_scatter | solution.py:169
  171.6 5.9 %copy-start.26 = (bf16[512,256]{1,0:T(8,128)(2,1)S(1)}, bf16[512,256]{1,0:T(8,128)(2,1)}, u32[]{:S(2)}) copy-start(bf16[512,256]{1,0:T(8,128)(2,1)} %copy.124) | copy-start | bytes 786436
  178.3 187.9 %reduce-scatter.8.cloned.1.call-start = ((), (), s32[]{:S(2)}) async-start(), calls=%async_computation.9 | async-start | bytes 6758400 | tf_op jit(solution)/shard_map/reduce_scatter | solution.py:176
  186.7 8.1 %copy-start.27 = (bf16[512,256]{0,1:T(8,128)(2,1)S(1)}, bf16[512,256]{0,1:T(8,128)(2,1)}, u32[]{:S(2)}) copy-start(bf16[512,256]{0,1:T(8,128)(2,1)} %copy.100) | copy-start | bytes 786436
  199.9 7.9 %copy-start.43 = (s32[512]{0:T(512)S(1)}, s32[512]{0:T(512)}, u32[]{:S(2)}) copy-start(s32[512]{0:T(512)} %get-tuple-element.27) | copy-start | bytes 6148
  199.9 67.0 %all-to-all-start.2 = ((bf16[32,16,1280]{2,1,0:T(8,128)(2,1)}), bf16[32,16,1280]{2,1,0:T(8,128)(2,1)}, u32[]{:S(2)}, u32[]{:S(2)}) async-start(bf16[32,16,1280]{2,1,0:T(8,128)(2,1)} %bitcast.69), calls=%async_computation.2 | async-start | bytes 2621440 | tf_op jit(solution)/shard_map/all_to_all | solution.py:192
  266.9 99.3 %copy-start.1 = (bf16[1280,1280]{1,0:T(8,128)(2,1)S(1)}, bf16[1280,1280]{1,0:T(8,128)(2,1)}, u32[]{:S(2)}) copy-start(bf16[1280,1280]{1,0:T(8,128)(2,1)} %param.12) | copy-start | bytes 9830404
  (35 other events, 93.7 us)
Sparse Core Ops, SparseCore 0:
  12.5 51.9 all-gather.1
  147.4 34.2 reduce-scatter.5
  184.6 31.0 reduce-scatter.3
  218.4 147.7 reduce-scatter.7
